TPU v7x, 256 devices: a whole 4x4x8 slice. The times are simulated.
256 devices in a mesh: gx: 8 (over z), gy: 16 (over y, x), sa: 2 (over core).
Axes of the slice: x: 4, y: 4, z: 8, core: 2. Of those that a mesh axis runs over, the one named last changes fastest.
Arguments:
- field: float32 [33, 32, 672, 256], P(None, 'gx', 'gy', 'sa'), as said below
- start: float32 [33, 16], replicated, may hold values from -1 to 1
Outputs:
- basis: float32 [33, 16], replicated
- gram_two: float32 [672, 672], P('gy', ('gx', 'sa'))
Inputs may be any that keep to these rules, and one draw needn't show every extreme that they name: `field`: every entry is finite; species differ in scale.
All inputs are finite; a program needn't handle non-finite values.
Results may differ from a plain program's by a relative error of at most 0.0003.
Values sent between devices are 32-bit elements; how exact they have to be, the bound alone decides.
A program may use at most 128 MiB of HBM per device.

v0:
```python
import jax
import jax.numpy as jnp
from jax import lax
from jax.sharding import PartitionSpec as P

ITERS = 4
HIGH = lax.Precision.HIGHEST


def orth(block):
    inner = jnp.dot(block.T, block, precision=HIGH, preferred_element_type=jnp.float32)
    lower = jnp.linalg.cholesky(inner)
    return jax.scipy.linalg.solve_triangular(lower, block.T, lower=True).T


def leading(gram, start, rounds):
    basis = orth(orth(start))
    for step in range(rounds):
        basis = orth(orth(jnp.dot(gram, basis, precision=HIGH, preferred_element_type=jnp.float32)))
    return basis


def project(basis, data):
    return jnp.einsum("sr,sxyz->rxyz", basis, data, precision=HIGH)


def line_gram(left, right):
    return jnp.einsum("rxiz,rxjz->ij", left, right, precision=HIGH)


def on_device(field, start):
    species, cells_x, cells_y, cells_z = field.shape
    ranks = start.shape[1]
    total_x = cells_x * lax.axis_size("gx")
    total_y = cells_y * lax.axis_size("gy")
    total_z = cells_z * lax.axis_size("sa")
    flat = field.reshape(species, -1)
    partial_gram = jnp.dot(flat, flat.T, precision=HIGH, preferred_element_type=jnp.float32)
    species_gram = lax.psum(partial_gram, ("gx", "gy", "sa")) / (total_x * total_y * total_z)
    basis = leading(species_gram, start, ITERS)
    core = project(basis, field)
    part_block = line_gram(core, lax.all_gather(core, "gy", axis=2, tiled=True))
    block = lax.psum_scatter(part_block, ("gx", "sa"), scatter_dimension=1, tiled=True) / (
        ranks * total_x * total_z
    )
    return (basis, block)


def solution(mesh):
    in_specs = (P(None, "gx", "gy", "sa"), P())
    out_specs = (P(), P("gy", ("gx", "sa")))
    return jax.shard_map(
        on_device, mesh=mesh, in_specs=in_specs, out_specs=out_specs, check_vma=False
    )
```

profile of v0, /device:TPU:1, one launch (start us, length us, event | category | flops | bytes accessed | tf_op | source)
XLA Modules:
  0.0 422.5 jit_solution(17980562996375337005)
XLA Ops:
  8.1 1.5 cholesky.164
  10.9 1.2 custom-call.14
  12.5 1.5 cholesky.175
  15.3 1.2 custom-call.15
  16.8 6.2 %fusion.12 = f32[33,33]{1,0:T(8,128)S(1)} fusion(f32[33,4,42,128]{3,1,2,0:T(4,128)} %param.5), kind=kOutput, calls=%fused_computation.8 | convolution fusion | flops 281014272 | bytes 2842884 | tf_op jit(solution)/shard_map/dot_general | solution.py:38
  22.9 81.5 %psum.7 = f32[33,33]{1,0:T(8,128)S(1)} all-reduce(f32[33,33]{1,0:T(8,128)S(1)} %fusion.12), channel_id=1, replica_groups=mesh['gx'=8,'gy'=16,'sa'=2] {'gx','gy','sa'}, use_global_device_ids=true, to_apply=%region_0.0 | all-reduce | flops 1089 | bytes 8712 | tf_op jit(solution)/shard_map/psum | solution.py:39
  104.8 1.5 cholesky.186
  107.6 1.2 custom-call.16
  109.3 1.5 cholesky.197
  112.1 1.2 custom-call.17
  113.9 1.5 cholesky.208
  116.7 1.2 custom-call.18
  118.4 1.5 cholesky.219
  121.2 1.2 custom-call.19
  123.0 1.5 cholesky.230
  125.8 1.2 custom-call.20
  127.4 1.5 cholesky.241
  132.0 1.5 cholesky.252
  136.5 1.5 cholesky.263
  140.8 3.4 fusion.2
  144.4 138.0 %all-gather.2.cloned.1.call-done = f32[16,4,672,128]{3,0,2,1:T(8,128)} async-done(((f32[16,4,42,128]{3,0,2,1:T(8,128)}), f32[16,4,672,128]{3,0,2,1:T(8,128)}) %all-gather.2.cloned.1.call-update) | async-done | bytes 22020112 | tf_op jit(solution)/shard_map/all_gather | solution.py:42
  282.4 29.2 %fusion.7 = f32[42,672]{1,0:T(8,128)} fusion(f32[16,4,672,128]{3,0,2,1:T(8,128)} %all-gather.2.cloned.1.call-done, f32[16,4,42,128]{3,0,2,1:T(8,128)} %fusion.2), kind=kOutput, calls=%fused_computation.7 | convolution fusion | flops 2774532096 | bytes 23509248 | tf_op jit(solution)/shard_map/rxiz,rxjz->ij/dot_general | solution.py:28
  312.9 101.3 %all-reduce.3.cloned.1.call-done = f32[42,672]{1,0:T(8,128)} async-done(((f32[42,672]{1,0:T(8,128)}), f32[42,672]{1,0:T(8,128)}) %all-reduce.3.cloned.1.call-update) | async-done | bytes 112912
  414.2 1.5 dynamic-slice_multiply_fusion
  (90 shorter events, 23.3 us)
Async XLA Ops:
  7.2 0.7 copy-start
  7.2 133.6 %copy-start.1 = (f32[33,4,42,128]{3,1,2,0:T(4,128)S(1)}, f32[33,4,42,128]{3,1,2,0:T(4,128)}, u32[]{:S(2)}) copy-start(f32[33,4,42,128]{3,1,2,0:T(4,128)} %param.5) | copy-start | bytes 8515588
  7.2 275.2 %all-gather.2.cloned.1.call-start = ((), (), s32[]{:S(2)}) async-start(), calls=%async_computation | async-start | bytes 23396352 | tf_op jit(solution)/shard_map/all_gather | solution.py:42
  140.7 3.4 copy-start.2
  144.2 167.4 %copy-start.3 = (u32[256]{0:T(256)S(1)}, u32[256]{0:T(256)}, u32[]{:S(2)}) copy-start(u32[256]{0:T(256)} %constant.40) | copy-start | bytes 3076
  144.2 270.0 %all-reduce.3.cloned.1.call-start = ((), (), s32[]{:S(2)}) async-start(), calls=%async_computation.1 | async-start | bytes 294912
Sparse Core Ops, SparseCore 0:
  144.3 138.0 all-gather.1
  311.7 102.3 all-reduce.2
where the time goes:
time: 423 us; the launch traced here: 422 us
  waiting for transfers between devices  239 us (57%)
  blocking collectives  81.5 us (19%)
  matrix products  42.7 us (10%)
  other arithmetic  41.8 us (10%)
  between operations  14.9 us (4%)
    all_gather x1, waiting for transfers between devices, on_device(): part_block = line_gram(core, lax.all_gather(core, 'gy', axis=2, tiled=True))  138 us
    unnamed x3, waiting for transfers between devices  101 us
    psum x1, blocking collectives, on_device(): lax.psum(partial_gram, ('gx', 'gy', 'sa')) / (total_x * total_y * total_z)  81.5 us
    dot_general x1, matrix products, line_gram(): return jnp.einsum('rxiz,rxjz->ij', left, right, precision=HIGH)  29.2 us
    another operation x30, other arithmetic, orth(): lower = jnp.linalg.cholesky(inner)  21.5 us
    another operation x20, other arithmetic, orth(): return jax.scipy.linalg.solve_triangular(lower, block.T, lower=True).T  18.8 us
  transfers between devices with their start and end apart: 2, of which 2 were waited for; matrix products, arithmetic and copies ran while one was open for 0% of the time, Pallas kernels for 0%

commit v1 on v0

--- a/solution.py
+++ b/solution.py
@@ -36,7 +36,9 @@
     total_z = cells_z * lax.axis_size("sa")
     flat = field.reshape(species, -1)
     partial_gram = jnp.dot(flat, flat.T, precision=HIGH, preferred_element_type=jnp.float32)
-    species_gram = lax.psum(partial_gram, ("gx", "gy", "sa")) / (total_x * total_y * total_z)
+    species_gram = lax.all_gather(partial_gram, ("gx", "gy", "sa")).sum(axis=0) / (
+        total_x * total_y * total_z
+    )
     basis = leading(species_gram, start, ITERS)
     core = project(basis, field)
     part_block = line_gram(core, lax.all_gather(core, "gy", axis=2, tiled=True))

time: 423 us -> 457 us (1.080)
  waiting for transfers between devices: 239 us -> 352 us
  blocking collectives: 81.5 us -> 0 us
    all_gather x0 -> x1, waiting for transfers between devices: none -> 112 us  [on_device(): lax.all_gather(partial_gram, ('gx', 'gy', 'sa')).sum(axis=0)]
    psum x1 -> x0, blocking collectives: 81.5 us -> none  [on_device(): lax.psum(partial_gram, ('gx', 'gy', 'sa')) / (total_x * total_y * total_z)]
    unnamed x3 -> x4, waiting for transfers between devices: 101 us -> 101 us
  transfers between devices with their start and end apart: 2 -> 3, of which waited for: 2 -> 3; matrix products, arithmetic and copies ran while one was open for 0% -> 2% of each run, Pallas kernels for 0% -> 0%
where the time goes in v1:
time: 457 us
  waiting for transfers between devices  352 us (77%)
  other arithmetic  44.8 us (10%)
  matrix products  43.3 us (9%)
  between operations  14.6 us (3%)
    all_gather x1, waiting for transfers between devices, on_device(): part_block = line_gram(core, lax.all_gather(core, 'gy', axis=2, tiled=True))  140 us
    all_gather x1, waiting for transfers between devices, on_device(): lax.all_gather(partial_gram, ('gx', 'gy', 'sa')).sum(axis=0)  112 us
    unnamed x4, waiting for transfers between devices  101 us
    dot_general x1, matrix products, line_gram(): return jnp.einsum('rxiz,rxjz->ij', left, right, precision=HIGH)  29.2 us
    another operation x30, other arithmetic, orth(): lower = jnp.linalg.cholesky(inner)  21.5 us
    another operation x20, other arithmetic, orth(): return jax.scipy.linalg.solve_triangular(lower, block.T, lower=True).T  18.8 us
  transfers between devices with their start and end apart: 3, of which 3 were waited for; matrix products, arithmetic and copies ran while one was open for 2% of the time, Pallas kernels for 0%

profile of v1, /device:TPU:1, one launch (start us, length us, event | category | flops | bytes accessed | tf_op | source)
XLA Modules:
  0.0 456.8 jit_solution(11824041834173788963)
XLA Ops:
  7.2 6.8 %fusion.12 = f32[1,33,33]{2,1,0:T(8,128)} fusion(f32[33,4,42,128]{3,1,2,0:T(4,128)} %param.5), kind=kOutput, calls=%fused_computation.8 | convolution fusion | flops 281014272 | bytes 2842884 | tf_op jit(solution)/shard_map/dot_general | solution.py:38
  14.3 1.5 cholesky.164
  17.1 1.2 custom-call.14
  18.7 1.5 cholesky.175
  21.5 1.2 custom-call.15
  23.0 111.5 %all-gather.7.cloned.1.call-done = f32[256,33,33]{2,1,0:T(8,128)} async-done(((f32[1,33,33]{2,1,0:T(8,128)}), f32[256,33,33]{2,1,0:T(8,128)}) %all-gather.7.cloned.1.call-update) | async-done | bytes 1115152 | tf_op jit(solution)/shard_map/all_gather | solution.py:39
  134.5 3.0 reduce_sum.9
  137.8 1.5 cholesky.186
  140.6 1.2 custom-call.16
  142.3 1.5 cholesky.197
  145.1 1.2 custom-call.17
  146.9 1.5 cholesky.208
  149.7 1.2 custom-call.18
  151.3 1.5 cholesky.219
  154.2 1.2 custom-call.19
  156.0 1.5 cholesky.230
  160.4 1.5 cholesky.241
  165.0 1.5 cholesky.252
  169.5 1.5 cholesky.263
  173.8 3.4 fusion.2
  177.4 139.6 %all-gather.5.cloned.1.call-done = f32[16,4,672,128]{3,0,2,1:T(8,128)} async-done(((f32[16,4,42,128]{3,0,2,1:T(8,128)}), f32[16,4,672,128]{3,0,2,1:T(8,128)}) %all-gather.5.cloned.1.call-update) | async-done | bytes 22020112 | tf_op jit(solution)/shard_map/all_gather | solution.py:44
  317.1 29.2 %fusion.7 = f32[42,672]{1,0:T(8,128)} fusion(f32[16,4,672,128]{3,0,2,1:T(8,128)} %all-gather.5.cloned.1.call-done, f32[16,4,42,128]{3,0,2,1:T(8,128)} %fusion.2), kind=kOutput, calls=%fused_computation.7 | convolution fusion | flops 2774532096 | bytes 23509248 | tf_op jit(solution)/shard_map/rxiz,rxjz->ij/dot_general | solution.py:28
  347.5 101.3 %all-reduce.3.cloned.1.call-done = f32[42,672]{1,0:T(8,128)} async-done(((f32[42,672]{1,0:T(8,128)}), f32[42,672]{1,0:T(8,128)}) %all-reduce.3.cloned.1.call-update) | async-done | bytes 112912
  448.8 1.5 dynamic-slice_multiply_fusion
  (93 shorter events, 24.0 us)
Async XLA Ops:
  7.2 6.9 %copy-start = (f32[33,16]{0,1:T(8,128)S(1)}, f32[33,16]{0,1:T(8,128)}, u32[]{:S(2)}) copy-start(f32[33,16]{0,1:T(8,128)} %param.6) | copy-start | bytes 6340
  7.2 127.3 %all-gather.7.cloned.1.call-start = ((), (), s32[]{:S(2)}) async-start(), calls=%async_computation.1 | async-start | bytes 5263360 | tf_op jit(solution)/shard_map/all_gather | solution.py:39
  14.0 303.1 %all-gather.5.cloned.1.call-start = ((), (), s32[]{:S(2)}) async-start(), calls=%async_computation | async-start | bytes 23396352 | tf_op jit(solution)/shard_map/all_gather | solution.py:44
  23.0 150.8 %copy-start.1 = (f32[33,4,42,128]{3,1,2,0:T(4,128)S(1)}, f32[33,4,42,128]{3,1,2,0:T(4,128)}, u32[]{:S(2)}) copy-start(f32[33,4,42,128]{3,1,2,0:T(4,128)} %param.5) | copy-start | bytes 8515588
  173.7 3.4 copy-start.2
  177.2 169.1 %copy-start.3 = (u32[256]{0:T(256)S(1)}, u32[256]{0:T(256)}, u32[]{:S(2)}) copy-start(u32[256]{0:T(256)} %constant.42) | copy-start | bytes 3076
  177.2 271.6 %all-reduce.3.cloned.1.call-start = ((), (), s32[]{:S(2)}) async-start(), calls=%async_computation.2 | async-start | bytes 294912
Sparse Core Ops, SparseCore 0:
  14.1 120.2 all-gather.6
  177.3 139.7 all-gather.4
  346.4 102.3 all-reduce.2
